TPU v7x, 1024 devices: a whole 4x4x32 slice. The times are simulated.
1024 devices in a mesh: row: 16 (over y, x), col: 64 (over z, core).
Axes of the slice: x: 4, y: 4, z: 32, core: 2. Of those that a mesh axis runs over, the one named last changes fastest.
Arguments:
- evecs: float32 [8192, 8192], P('row', 'col'), may hold values from -6 to 6
- offsets: int32 [4, 2], replicated, may hold values from 0 to 127, as said below
- refl: float32 [4, 2, 64, 64, 192], P(None, None, 'row', 'col'), may hold values from -6 to 6, as said below
Outputs:
- rotated: float32 [8192, 8192], P('row', 'col')
Inputs may be any that keep to these rules, and one draw needn't show every extreme that they name: Within each round and sweep the windows start at offsets plus multiples of 128; some entry is 0 and some is 127 in every draw. `refl`: each block's triangular factor T is the inverse of the strictly upper part of V^T V plus half its diagonal, so that I - V T V^T is orthogonal.
All inputs are finite; a program needn't handle non-finite values.
Results may differ from a plain program's by a relative error of at most 0.0003.
Values sent between devices are 32-bit elements; how exact they have to be, the bound alone decides.
A program may use at most 32 MiB of HBM per device.

v0:
```python
import jax
import jax.numpy as jnp
from jax import lax
from jax.sharding import PartitionSpec as P

WINDOW_ROWS = 128
SWEEP_ROUNDS = 4


def shifted(block, axis, distance):
    devices = range(lax.axis_size(axis))
    route = [(i - distance, i) for i in devices if i - distance in devices]
    return lax.ppermute(block, axis, route)


def apply_blocks(window, reflect, factor, extra):
    proj = jnp.einsum("kjw,kwc->kjc", reflect, window, precision=lax.Precision.HIGHEST) + extra
    scaled = jnp.einsum("kij,kjc->kic", factor, proj, precision=lax.Precision.HIGHEST)
    updated = window - jnp.einsum("kjw,kjc->kwc", reflect, scaled, precision=lax.Precision.HIGHEST)
    return (updated, scaled)


def shards(evecs, offsets, refl):
    rows, cols = evecs.shape
    nwin = rows // WINDOW_ROWS
    place = lax.axis_index("row")
    for rnd in range(SWEEP_ROUNDS):
        blocks = lax.all_gather(refl[rnd], "col", axis=2, tiled=True)
        for sweep in range(2):
            start = offsets[rnd, sweep]
            reflect = blocks[sweep, :, :, :WINDOW_ROWS]
            factor = blocks[sweep, :, :, WINDOW_ROWS:]
            below = shifted(evecs[:WINDOW_ROWS], "row", -1)
            extended = jnp.concatenate([evecs, below], 0)
            window = lax.dynamic_slice_in_dim(extended, start, rows, 0).reshape(
                nwin, WINDOW_ROWS, cols
            )
            updated, unused = apply_blocks(window, reflect, factor, 0.0)
            extended = lax.dynamic_update_slice_in_dim(
                extended, updated.reshape(rows, cols), start, 0
            )
            above = shifted(extended[rows:], "row", 1)
            lines = lax.broadcasted_iota(jnp.int32, (WINDOW_ROWS, 1), 0)
            taking = (lines < start) & (place > 0)
            head = jnp.where(taking, above, extended[:WINDOW_ROWS])
            evecs = jnp.concatenate([head, extended[WINDOW_ROWS:rows]], 0)
    return evecs


def solution(mesh):
    placed = (P("row", "col"), P(), P(None, None, "row", "col", None))
    return jax.shard_map(
        shards, mesh=mesh, in_specs=placed, out_specs=P("row", "col"), check_vma=False
    )
```

profile of v0, /device:TPU:24, one launch (start us, length us, event | category | flops | bytes accessed | tf_op | source)
XLA Modules:
  0.0 370.6 jit_solution(1090838469562898055)
XLA Ops:
  0.9 5.0 %collective-permute-start = (f32[128,128]{1,0:T(8,128)S(1)}, f32[128,128]{1,0:T(8,128)S(1)}, u32[]{:S(2)}, u32[]{:S(2)}) collective-permute-start(f32[128,128]{1,0:T(8,128)S(1)} %slice.167), channel_id=1, source_target_pairs={{64,0},{128,64},{192,128},{256,192},{320,256},{384,320},{448,384},... | collective-permute-start | bytes 196616 | tf_op jit(solution)/shard_map/ppermute | solution.py:13
  7.9 70.2 %all-gather = f32[1,2,4,64,192]{4,2,1,0,3:T(4,128)S(1)} all-gather(f32[1,2,4,1,192]{4,2,1,0,3:T(4,128)S(1)} %copy.12), channel_id=2, replica_groups=mesh['row'=16,'col'=64] {'col'}, dimensions={3}, use_global_device_ids=true | all-gather | bytes 399360 | tf_op jit(solution)/shard_map/all_gather | solution.py:28
  82.2 1.9 collective-permute-start.1
  84.8 5.7 %collective-permute-done.1 = f32[128,128]{1,0:T(8,128)S(1)} collective-permute-done((f32[128,128]{1,0:T(8,128)S(1)}, f32[128,128]{1,0:T(8,128)S(1)}, u32[]{:S(2)}, u32[]{:S(2)}) %collective-permute-start.1) | collective-permute-done | bytes 65568 | tf_op jit(solution)/shard_map/ppermute | solution.py:13
  90.6 1.9 collective-permute-start.2
  94.3 2.5 collective-permute-done.2
  99.9 1.9 collective-permute-start.3
  102.4 5.8 %collective-permute-done.3 = f32[128,128]{1,0:T(8,128)S(1)} collective-permute-done((f32[128,128]{1,0:T(8,128)S(1)}, f32[128,128]{1,0:T(8,128)S(1)}, u32[]{:S(2)}, u32[]{:S(2)}) %collective-permute-start.3) | collective-permute-done | bytes 65568 | tf_op jit(solution)/shard_map/ppermute | solution.py:13
  108.2 1.9 collective-permute-start.4
  110.2 53.5 %all-gather.1 = f32[1,2,4,64,192]{4,2,1,0,3:T(4,128)S(1)} all-gather(f32[1,2,4,1,192]{4,2,1,0,3:T(4,128)S(1)} %copy.13), channel_id=3, replica_groups=mesh['row'=16,'col'=64] {'col'}, dimensions={3}, use_global_device_ids=true | all-gather | bytes 399360 | tf_op jit(solution)/shard_map/all_gather | solution.py:28
  168.6 3.9 %collective-permute-start.5 = (f32[128,128]{1,0:T(8,128)S(1)}, f32[128,128]{1,0:T(8,128)S(1)}, u32[]{:S(2)}, u32[]{:S(2)}) collective-permute-start(f32[128,128]{1,0:T(8,128)S(1)} %slice.224), channel_id=1, source_target_pairs={{0,64},{64,128},{128,192},{192,256},{256,320},{320,384},{384,448},... | collective-permute-start | bytes 196616 | tf_op jit(solution)/shard_map/ppermute | solution.py:13
  173.1 3.8 %collective-permute-done.5 = f32[128,128]{1,0:T(8,128)S(1)} collective-permute-done((f32[128,128]{1,0:T(8,128)S(1)}, f32[128,128]{1,0:T(8,128)S(1)}, u32[]{:S(2)}, u32[]{:S(2)}) %collective-permute-start.5) | collective-permute-done | bytes 65568 | tf_op jit(solution)/shard_map/ppermute | solution.py:13
  177.0 1.9 collective-permute-start.6
  180.9 2.3 collective-permute-done.6
  186.2 1.9 collective-permute-start.7
  188.8 5.7 %collective-permute-done.7 = f32[128,128]{1,0:T(8,128)S(1)} collective-permute-done((f32[128,128]{1,0:T(8,128)S(1)}, f32[128,128]{1,0:T(8,128)S(1)}, u32[]{:S(2)}, u32[]{:S(2)}) %collective-permute-start.7) | collective-permute-done | bytes 65568 | tf_op jit(solution)/shard_map/ppermute | solution.py:13
  194.6 1.9 collective-permute-start.8
  196.5 55.4 %all-gather.2 = f32[1,2,4,64,192]{4,2,1,0,3:T(4,128)S(1)} all-gather(f32[1,2,4,1,192]{4,2,1,0,3:T(4,128)S(1)} %copy.14), channel_id=4, replica_groups=mesh['row'=16,'col'=64] {'col'}, dimensions={3}, use_global_device_ids=true | all-gather | bytes 399360 | tf_op jit(solution)/shard_map/all_gather | solution.py:28
  257.1 3.9 %collective-permute-start.9 = (f32[128,128]{1,0:T(8,128)S(1)}, f32[128,128]{1,0:T(8,128)S(1)}, u32[]{:S(2)}, u32[]{:S(2)}) collective-permute-start(f32[128,128]{1,0:T(8,128)S(1)} %slice.234), channel_id=1, source_target_pairs={{0,64},{64,128},{128,192},{192,256},{256,320},{320,384},{384,448},... | collective-permute-start | bytes 196616 | tf_op jit(solution)/shard_map/ppermute | solution.py:13
  261.7 3.8 %collective-permute-done.9 = f32[128,128]{1,0:T(8,128)S(1)} collective-permute-done((f32[128,128]{1,0:T(8,128)S(1)}, f32[128,128]{1,0:T(8,128)S(1)}, u32[]{:S(2)}, u32[]{:S(2)}) %collective-permute-start.9) | collective-permute-done | bytes 65568 | tf_op jit(solution)/shard_map/ppermute | solution.py:13
  265.6 2.1 collective-permute-start.10
  269.6 2.1 collective-permute-done.10
  274.8 1.9 collective-permute-start.11
  277.4 5.7 %collective-permute-done.11 = f32[128,128]{1,0:T(8,128)S(1)} collective-permute-done((f32[128,128]{1,0:T(8,128)S(1)}, f32[128,128]{1,0:T(8,128)S(1)}, u32[]{:S(2)}, u32[]{:S(2)}) %collective-permute-start.11) | collective-permute-done | bytes 65568 | tf_op jit(solution)/shard_map/ppermute | solution.py:13
  283.2 1.9 collective-permute-start.12
  285.1 53.5 %all-gather.3 = f32[1,2,4,64,192]{4,2,1,0,3:T(4,128)S(1)} all-gather(f32[1,2,4,1,192]{4,2,1,0,3:T(4,128)S(1)} %copy.15), channel_id=5, replica_groups=mesh['row'=16,'col'=64] {'col'}, dimensions={3}, use_global_device_ids=true | all-gather | bytes 399360 | tf_op jit(solution)/shard_map/all_gather | solution.py:28
  343.9 3.9 %collective-permute-start.13 = (f32[128,128]{1,0:T(8,128)S(1)}, f32[128,128]{1,0:T(8,128)S(1)}, u32[]{:S(2)}, u32[]{:S(2)}) collective-permute-start(f32[128,128]{1,0:T(8,128)S(1)} %slice.244), channel_id=1, source_target_pairs={{0,64},{64,128},{128,192},{192,256},{256,320},{320,384},{384,448},... | collective-permute-start | bytes 196616 | tf_op jit(solution)/shard_map/ppermute | solution.py:13
  348.5 3.8 %collective-permute-done.13 = f32[128,128]{1,0:T(8,128)S(1)} collective-permute-done((f32[128,128]{1,0:T(8,128)S(1)}, f32[128,128]{1,0:T(8,128)S(1)}, u32[]{:S(2)}, u32[]{:S(2)}) %collective-permute-start.13) | collective-permute-done | bytes 65568 | tf_op jit(solution)/shard_map/ppermute | solution.py:13
  352.3 1.9 collective-permute-start.14
  356.2 2.3 collective-permute-done.14
  361.5 1.9 collective-permute-start.15
  364.1 5.7 %collective-permute-done.15 = f32[128,128]{1,0:T(8,128)S(1)} collective-permute-done((f32[128,128]{1,0:T(8,128)S(1)}, f32[128,128]{1,0:T(8,128)S(1)}, u32[]{:S(2)}, u32[]{:S(2)}) %collective-permute-start.15) | collective-permute-done | bytes 65568 | tf_op jit(solution)/shard_map/ppermute | solution.py:13
  (103 shorter events, 33.0 us)
Async XLA Ops:
  0.0 7.9 %copy-start.1 = (f32[4,2,4,1,192]{4,3,2,1,0:T(1,128)S(1)}, f32[4,2,4,1,192]{4,3,2,1,0:T(1,128)}, u32[]{:S(2)}) copy-start(f32[4,2,4,1,192]{4,3,2,1,0:T(1,128)} %param.5) | copy-start | bytes 73732
  0.9 5.0 %copy-start.2 = (s32[4,2]{0,1:T(2,128)S(1)}, s32[4,2]{0,1:T(2,128)}, u32[]{:S(2)}) copy-start(s32[4,2]{0,1:T(2,128)} %param.4) | copy-start | bytes 100
  0.9 78.3 %collective-permute-start = (f32[128,128]{1,0:T(8,128)S(1)}, f32[128,128]{1,0:T(8,128)S(1)}, u32[]{:S(2)}, u32[]{:S(2)}) collective-permute-start(f32[128,128]{1,0:T(8,128)S(1)} %slice.167), channel_id=1, source_target_pairs={{64,0},{128,64},{192,128},{256,192},{320,256},{384,320},{448,384},... | collective-permute-start | bytes 196616 | tf_op jit(solution)/shard_map/ppermute | solution.py:13
  78.2 0.9 copy-start
  82.2 8.3 %collective-permute-start.1 = (f32[128,128]{1,0:T(8,128)S(1)}, f32[128,128]{1,0:T(8,128)S(1)}, u32[]{:S(2)}, u32[]{:S(2)}) collective-permute-start(f32[128,128]{1,0:T(8,128)S(1)} %slice.214), channel_id=1, source_target_pairs={{0,64},{64,128},{128,192},{192,256},{256,320},{320,384},{384,448},... | collective-permute-start | bytes 196616 | tf_op jit(solution)/shard_map/ppermute | solution.py:13
  90.6 6.2 %collective-permute-start.2 = (f32[128,128]{1,0:T(8,128)S(1)}, f32[128,128]{1,0:T(8,128)S(1)}, u32[]{:S(2)}, u32[]{:S(2)}) collective-permute-start(f32[128,128]{1,0:T(8,128)S(1)} %slice_select_fusion.7), channel_id=1, source_target_pairs={{64,0},{128,64},{192,128},{256,192},{320,256},{384,320},{448,384},... | collective-permute-start | bytes 196616 | tf_op jit(solution)/shard_map/ppermute | solution.py:13
  99.9 8.3 %collective-permute-start.3 = (f32[128,128]{1,0:T(8,128)S(1)}, f32[128,128]{1,0:T(8,128)S(1)}, u32[]{:S(2)}, u32[]{:S(2)}) collective-permute-start(f32[128,128]{1,0:T(8,128)S(1)} %slice.219), channel_id=1, source_target_pairs={{0,64},{64,128},{128,192},{192,256},{256,320},{320,384},{384,448},... | collective-permute-start | bytes 196616 | tf_op jit(solution)/shard_map/ppermute | solution.py:13
  108.2 57.3 %collective-permute-start.4 = (f32[128,128]{1,0:T(8,128)S(1)}, f32[128,128]{1,0:T(8,128)S(1)}, u32[]{:S(2)}, u32[]{:S(2)}) collective-permute-start(f32[128,128]{1,0:T(8,128)S(1)} %slice_select_fusion.6), channel_id=1, source_target_pairs={{64,0},{128,64},{192,128},{256,192},{320,256},{384,320},{448,384},... | collective-permute-start | bytes 196616 | tf_op jit(solution)/shard_map/ppermute | solution.py:13
  168.6 8.3 %collective-permute-start.5 = (f32[128,128]{1,0:T(8,128)S(1)}, f32[128,128]{1,0:T(8,128)S(1)}, u32[]{:S(2)}, u32[]{:S(2)}) collective-permute-start(f32[128,128]{1,0:T(8,128)S(1)} %slice.224), channel_id=1, source_target_pairs={{0,64},{64,128},{128,192},{192,256},{256,320},{320,384},{384,448},... | collective-permute-start | bytes 196616 | tf_op jit(solution)/shard_map/ppermute | solution.py:13
  177.0 6.2 %collective-permute-start.6 = (f32[128,128]{1,0:T(8,128)S(1)}, f32[128,128]{1,0:T(8,128)S(1)}, u32[]{:S(2)}, u32[]{:S(2)}) collective-permute-start(f32[128,128]{1,0:T(8,128)S(1)} %slice_select_fusion.5), channel_id=1, source_target_pairs={{64,0},{128,64},{192,128},{256,192},{320,256},{384,320},{448,384},... | collective-permute-start | bytes 196616 | tf_op jit(solution)/shard_map/ppermute | solution.py:13
  186.2 8.3 %collective-permute-start.7 = (f32[128,128]{1,0:T(8,128)S(1)}, f32[128,128]{1,0:T(8,128)S(1)}, u32[]{:S(2)}, u32[]{:S(2)}) collective-permute-start(f32[128,128]{1,0:T(8,128)S(1)} %slice.229), channel_id=1, source_target_pairs={{0,64},{64,128},{128,192},{192,256},{256,320},{320,384},{384,448},... | collective-permute-start | bytes 196616 | tf_op jit(solution)/shard_map/ppermute | solution.py:13
  194.6 59.5 %collective-permute-start.8 = (f32[128,128]{1,0:T(8,128)S(1)}, f32[128,128]{1,0:T(8,128)S(1)}, u32[]{:S(2)}, u32[]{:S(2)}) collective-permute-start(f32[128,128]{1,0:T(8,128)S(1)} %slice_select_fusion.4), channel_id=1, source_target_pairs={{64,0},{128,64},{192,128},{256,192},{320,256},{384,320},{448,384},... | collective-permute-start | bytes 196616 | tf_op jit(solution)/shard_map/ppermute | solution.py:13
  257.1 8.3 %collective-permute-start.9 = (f32[128,128]{1,0:T(8,128)S(1)}, f32[128,128]{1,0:T(8,128)S(1)}, u32[]{:S(2)}, u32[]{:S(2)}) collective-permute-start(f32[128,128]{1,0:T(8,128)S(1)} %slice.234), channel_id=1, source_target_pairs={{0,64},{64,128},{128,192},{192,256},{256,320},{320,384},{384,448},... | collective-permute-start | bytes 196616 | tf_op jit(solution)/shard_map/ppermute | solution.py:13
  265.6 6.2 %collective-permute-start.10 = (f32[128,128]{1,0:T(8,128)S(1)}, f32[128,128]{1,0:T(8,128)S(1)}, u32[]{:S(2)}, u32[]{:S(2)}) collective-permute-start(f32[128,128]{1,0:T(8,128)S(1)} %slice_select_fusion.3), channel_id=1, source_target_pairs={{64,0},{128,64},{192,128},{256,192},{320,256},{384,320},{448,384},... | collective-permute-start | bytes 196616 | tf_op jit(solution)/shard_map/ppermute | solution.py:13
  274.8 8.3 %collective-permute-start.11 = (f32[128,128]{1,0:T(8,128)S(1)}, f32[128,128]{1,0:T(8,128)S(1)}, u32[]{:S(2)}, u32[]{:S(2)}) collective-permute-start(f32[128,128]{1,0:T(8,128)S(1)} %slice.239), channel_id=1, source_target_pairs={{0,64},{64,128},{128,192},{192,256},{256,320},{320,384},{384,448},... | collective-permute-start | bytes 196616 | tf_op jit(solution)/shard_map/ppermute | solution.py:13
  283.2 57.5 %collective-permute-start.12 = (f32[128,128]{1,0:T(8,128)S(1)}, f32[128,128]{1,0:T(8,128)S(1)}, u32[]{:S(2)}, u32[]{:S(2)}) collective-permute-start(f32[128,128]{1,0:T(8,128)S(1)} %slice_select_fusion.2), channel_id=1, source_target_pairs={{64,0},{128,64},{192,128},{256,192},{320,256},{384,320},{448,384},... | collective-permute-start | bytes 196616 | tf_op jit(solution)/shard_map/ppermute | solution.py:13
  343.9 8.3 %collective-permute-start.13 = (f32[128,128]{1,0:T(8,128)S(1)}, f32[128,128]{1,0:T(8,128)S(1)}, u32[]{:S(2)}, u32[]{:S(2)}) collective-permute-start(f32[128,128]{1,0:T(8,128)S(1)} %slice.244), channel_id=1, source_target_pairs={{0,64},{64,128},{128,192},{192,256},{256,320},{320,384},{384,448},... | collective-permute-start | bytes 196616 | tf_op jit(solution)/shard_map/ppermute | solution.py:13
  352.3 6.2 %collective-permute-start.14 = (f32[128,128]{1,0:T(8,128)S(1)}, f32[128,128]{1,0:T(8,128)S(1)}, u32[]{:S(2)}, u32[]{:S(2)}) collective-permute-start(f32[128,128]{1,0:T(8,128)S(1)} %slice_select_fusion.1), channel_id=1, source_target_pairs={{64,0},{128,64},{192,128},{256,192},{320,256},{384,320},{448,384},... | collective-permute-start | bytes 196616 | tf_op jit(solution)/shard_map/ppermute | solution.py:13
  361.5 8.3 %collective-permute-start.15 = (f32[128,128]{1,0:T(8,128)S(1)}, f32[128,128]{1,0:T(8,128)S(1)}, u32[]{:S(2)}, u32[]{:S(2)}) collective-permute-start(f32[128,128]{1,0:T(8,128)S(1)} %slice.249), channel_id=1, source_target_pairs={{0,64},{64,128},{128,192},{192,256},{256,320},{320,384},{384,448},... | collective-permute-start | bytes 196616 | tf_op jit(solution)/shard_map/ppermute | solution.py:13
where the time goes:
time: 372 us; the launch traced here: 371 us
  blocking collectives  233 us (63%)
  waiting for transfers between devices  49.2 us (13%)
  starting transfers between devices  40 us (11%)
  between operations  15.8 us (4%)
  matrix products  14.2 us (4%)
  local copies, waits for them, and re-layouts  12.2 us (3%)
  other arithmetic  6.56 us (2%)
    all_gather x4, blocking collectives, shards(): blocks = lax.all_gather(refl[rnd], 'col', axis=2, tiled=True)  233 us
    ppermute x16, waiting for transfers between devices, shifted(): return lax.ppermute(block, axis, route)  49.2 us
    ppermute x16, starting transfers between devices, shifted(): return lax.ppermute(block, axis, route)  40 us
    dynamic_update_slice x8, local copies, waits for them, and re-layouts, shards(): lax.dynamic_update_slice_in_dim(extended, updated.reshape(rows, cols), st...  9.46 us
  transfers between devices with their start and end apart: 16, of which 12 were waited for; matrix products, arithmetic and copies ran while one was open for 2% of the time, Pallas kernels for 0%

commit v1 on v0

v1 whole, which is shorter than its diff:
```python
import functools

import jax
import jax.numpy as jnp
from jax import lax
from jax.experimental import pallas as pl
from jax.experimental.pallas import tpu as pltpu
from jax.sharding import PartitionSpec as P

WR = 128
NREF = 64
ROUNDS = 4
NWIN = 4
NCOL = 128
STRIDE = 2
CHUNKS = 2
CROWS = 24
SROWS = CHUNKS * CROWS
MESH = pl.DeviceIdType.MESH
F32 = jnp.float32
BF16 = jnp.bfloat16


def split(x):
    hi = x.astype(BF16)
    return hi, (x - hi.astype(F32)).astype(BF16)


def dot3(a, b, dims):
    def one(x, y):
        return lax.dot_general(x, y, (dims, ((), ())), preferred_element_type=F32)

    (ah, al), (bh, bl) = a, b
    return one(ah, bh) + (one(ah, bl) + one(al, bh))


def kernel(
    nrow, nz, off_ref, refl_ref, ev_ref, out_ref,
    gath, own0, own1, lo0, lo1, hi0, hi1, hmat_hi, hmat_lo,
    zsend, zrecv, psend, precv, xsend, xrecv, lsem,
):
    p = lax.axis_index("row")
    j = lax.axis_index("col")
    z, c = j // 2, j % 2
    partner = z * 2 + (1 - c)
    own, lo, hi = (own0, own1), (lo0, lo1), (hi0, hi1)

    def chip(d):
        return lax.rem(z + d + 2 * nz, nz)

    barrier = pltpu.get_barrier_semaphore()
    for d in [x for x in range(-STRIDE, STRIDE + 1) if x]:
        pl.semaphore_signal(barrier, inc=1, device_id={"col": chip(d) * 2 + c}, device_id_type=MESH)
    pl.semaphore_signal(barrier, inc=1, device_id={"col": partner}, device_id_type=MESH)

    @pl.when(p > 0)
    def _():
        pl.semaphore_signal(barrier, inc=1, device_id={"row": p - 1}, device_id_type=MESH)

    @pl.when(p < nrow - 1)
    def _():
        pl.semaphore_signal(barrier, inc=1, device_id={"row": p + 1}, device_id_type=MESH)

    local = [
        pltpu.make_async_copy(ev_ref, own0, lsem.at[0]),
        pltpu.make_async_copy(ev_ref.at[pl.ds(0, 2 * WR)], lo0.at[pl.ds(2 * WR, 2 * WR)], lsem.at[1]),
        pltpu.make_async_copy(ev_ref.at[pl.ds(2 * WR, 2 * WR)], hi0.at[pl.ds(0, 2 * WR)], lsem.at[2]),
    ]
    for copy in local:
        copy.start()

    def piece(rnd):
        return refl_ref[pl.ds(8 * rnd, 8), :WR]

    def factors(rnd):
        a = refl_ref[pl.ds(8 * rnd, 8), WR:]
        b = refl_ref[pl.ds(8 * rnd + 8, 8), WR:]
        return jnp.concatenate([a, b], 1)

    base = pl.multiple_of(j * SROWS, 8)
    for tile, value in enumerate((piece(0), factors(0), piece(1), piece(2), factors(2), piece(3))):
        gath[pl.ds(base + 8 * tile, 8), :value.shape[1]] = value
    for par in range(2):
        lo[par][pl.ds(0, WR), :] = jnp.zeros((WR, NCOL), F32)

    @pl.when(p == 0)
    def _():
        for par in range(2):
            lo[par][pl.ds(WR, WR), :] = jnp.zeros((WR, NCOL), F32)

    @pl.when(p == nrow - 1)
    def _():
        for par in range(2):
            hi[par][pl.ds(2 * WR, WR), :] = jnp.zeros((WR, NCOL), F32)

    pl.semaphore_wait(barrier, 2 * STRIDE + 1 + (p > 0).astype(jnp.int32) + (p < nrow - 1).astype(jnp.int32))

    def down(t):
        par = t % 2
        src = ev_ref.at[pl.ds(0, WR)] if t == 0 else lo[par].at[pl.ds(2 * WR, WR)]
        return pltpu.make_async_remote_copy(
            src, hi[par].at[pl.ds(2 * WR, WR)], xsend.at[0, par], xrecv.at[0, par],
            device_id={"row": p - 1}, device_id_type=MESH,
        )

    def up(t):
        par = t % 2
        return pltpu.make_async_remote_copy(
            hi[par].at[pl.ds(WR, WR)], lo[par].at[pl.ds(WR, WR)], xsend.at[1, par], xrecv.at[1, par],
            device_id={"row": p + 1}, device_id_type=MESH,
        )

    def if_below(f):
        pl.when(p > 0)(f)

    def if_above(f):
        pl.when(p < nrow - 1)(f)

    if_below(lambda: down(0).start())

    def rows_of(chip_index, core, q):
        at = (chip_index * 2 + core) * SROWS + q * CROWS
        return gath.at[pl.ds(pl.multiple_of(at, 8), CROWS)]

    def hop(way, d, q, reach):
        sgn = 1 - 2 * way
        part = rows_of(chip(-sgn * d), c, q)
        return pltpu.make_async_remote_copy(
            part, part, zsend.at[way, q, d + reach], zrecv.at[way, q, d + reach],
            device_id={"col": chip(sgn * reach) * 2 + c}, device_id_type=MESH,
        )

    def arrival(way, d, q):
        sgn = 1 - 2 * way
        part = rows_of(chip(-sgn * d), c, q)
        return pltpu.make_async_remote_copy(
            part, part, zsend.at[way, q, d], zrecv.at[way, q, d],
            device_id={"col": chip(sgn) * 2 + c}, device_id_type=MESH,
        )

    def across(src_chip, q):
        part = rows_of(src_chip, c, q)
        return pltpu.make_async_remote_copy(
            part, part, psend.at[q, src_chip], precv.at[q, src_chip],
            device_id={"col": partner}, device_id_type=MESH,
        )

    def from_partner(src_chip, q):
        part = rows_of(src_chip, 1 - c, q)
        return pltpu.make_async_remote_copy(
            part, part, psend.at[q, src_chip], precv.at[q, src_chip],
            device_id={"col": partner}, device_id_type=MESH,
        )

    def far(way, q):
        return nz // 2 if way == q else nz // 2 - 1

    def reaches(d, way, q, last):
        order = [STRIDE] + list(range(1, STRIDE))
        return [r for r in order if not last or d + r <= far(way, q)]

    def relay(d, last):
        for q in range(CHUNKS):
            for way in range(2):
                if not isinstance(d, int) or d > 0:
                    arrival(way, d, q).wait_recv()
                for r in reaches(d, way, q, last):
                    hop(way, d, q, r).start()
            if isinstance(d, int) and d == 0:
                across(z, q).start()
            else:
                for way in range(2):
                    across(chip((2 * way - 1) * d), q).start()

    def settle_step(d):
        for q in range(CHUNKS):
            for way in range(2):
                for r in range(1, STRIDE):
                    arrival(way, d + r, q).wait_recv()
                    across(chip((2 * way - 1) * (d + r)), q).start()

    half = nz // 2
    last_relay = half - STRIDE
    relay(0, last_relay == 0)

    def step(m, carry):
        relay(m * STRIDE, False)
        settle_step((m - 1) * STRIDE)
        return carry

    lax.fori_loop(1, last_relay // STRIDE, step, 0)
    relay(last_relay, True)
    if last_relay:
        settle_step(last_relay - STRIDE)
    for q in range(CHUNKS):
        for way in range(2):
            for d in range(last_relay + 1, far(way, q) + 1):
                arrival(way, d, q).wait_recv()
                across(chip((2 * way - 1) * d), q).start()

    def partner_done(q):
        def body(i, carry):
            from_partner(i, q).wait_recv()
            return carry
        lax.fori_loop(0, nz, body, 0)

    for copy in local:
        copy.wait()

    eye = (
        lax.broadcasted_iota(jnp.int32, (WR, WR), 0) == lax.broadcasted_iota(jnp.int32, (WR, WR), 1)
    ).astype(F32)

    def build(t):
        rnd, sweep = t // 2, t % 2
        vtile = (0, 2, 3, 5)[rnd]
        ttile = (1, 1, 4, 4)[rnd]
        for w in range(NWIN):
            row = sweep * NWIN + w
            vt = split(gath[pl.ds(8 * vtile + row, NREF, stride=SROWS), :])
            packed = gath[pl.ds(8 * ttile + row, NREF, stride=SROWS), :]
            tf = split(packed[:, NREF * (rnd % 2):NREF * (rnd % 2) + NREF])
            tv = split(dot3(tf, vt, ((1,), (0,))))
            h, l = split(eye - dot3(vt, tv, ((0,), (0,))))
            hmat_hi[t % 2, w] = h
            hmat_lo[t % 2, w] = l

    def apply(t, w, rows):
        e = split(rows)
        return dot3((hmat_hi[t % 2, w], hmat_lo[t % 2, w]), e, ((1,), (0,)))

    def offset(t):
        return off_ref[(t - 1) // 2, (t - 1) % 2] if t else 0

    lines = lax.broadcasted_iota(jnp.int32, (WR, NCOL), 0)
    partner_done(0)
    build(0)
    for t in range(1, 2 * ROUNDS + 1):
        old, new = (t - 1) % 2, t % 2
        shift = offset(t) - offset(t - 1)
        for w in (1, 2):
            got = apply(t - 1, w, own[old][pl.ds(shift + WR * w, WR), :])
            own[new][pl.ds(WR * w, WR), :] = got
            if w == 1:
                lo[new][pl.ds(3 * WR, WR), :] = got
            else:
                hi[new][pl.ds(0, WR), :] = got
        if t == ROUNDS:
            partner_done(1)
        if t < 2 * ROUNDS:
            build(t)
        if_above(lambda: down(t - 1).wait_recv())
        if t > 1:
            if_below(lambda: up(t - 1).wait_recv())
        if t > 2:
            if_below(lambda: down(t - 2).wait_send())
            if_above(lambda: up(t - 2).wait_send())
        elif t == 2:
            if_below(lambda: down(0).wait_send())

        @pl.when(p == 0)
        def _():
            lo[new][pl.ds(WR, WR), :] = lo[old][pl.ds(shift + WR, WR), :]

        got = apply(t - 1, 0, lo[old][pl.ds(shift + 2 * WR, WR), :])
        lo[new][pl.ds(2 * WR, WR), :] = got
        if t < 2 * ROUNDS:
            if_below(lambda: down(t).start())
        own[new][pl.ds(0, WR), :] = got
        got = apply(t - 1, 3, hi[old][pl.ds(shift + WR, WR), :])
        limit = jnp.where(p == nrow - 1, WR - offset(t), WR)
        got = jnp.where(lines < limit, got, 0.0)
        hi[new][pl.ds(WR, WR), :] = got
        if_above(lambda: up(t).start())
        own[new][pl.ds(3 * WR, WR), :] = got

    final = 2 * ROUNDS
    par = final % 2
    tail = pltpu.make_async_copy(own[par], out_ref.at[pl.ds(WR, NWIN * WR)], lsem.at[0])
    tail.start()
    if_below(lambda: up(final).wait_recv())
    head = pltpu.make_async_copy(lo[par].at[pl.ds(WR, WR)], out_ref.at[pl.ds(0, WR)], lsem.at[1])
    head.start()

    if_below(lambda: down(final - 1).wait_send())
    if_above(lambda: up(final - 1).wait_send())
    if_above(lambda: up(final).wait_send())

    def drain(i, carry):
        for q in range(CHUNKS):
            across(i, q).wait_send()
        return carry

    lax.fori_loop(0, nz, drain, 0)
    for q in range(CHUNKS):
        for way in range(2):
            def drain_z(d, carry, way=way, q=q):
                arrival(way, d, q).wait_send()
                return carry
            lax.fori_loop(1, far(way, q) + 1, drain_z, 0)
    tail.wait()
    head.wait()


def shards(evecs, offsets, refl):
    nrow, ncol = lax.axis_size("row"), lax.axis_size("col")
    nz = ncol // 2
    vec = lambda rows: pltpu.VMEM((rows, NCOL), F32)
    sem = pltpu.SemaphoreType.DMA
    reach = nz // 2 + 1
    spread = pl.pallas_call(
        functools.partial(kernel, nrow, nz),
        out_shape=jax.ShapeDtypeStruct(((NWIN + 1) * WR, NCOL), F32),
        in_specs=[
            pl.BlockSpec(memory_space=pltpu.SMEM),
            pl.BlockSpec(memory_space=pltpu.VMEM),
            pl.BlockSpec(memory_space=pl.ANY),
        ],
        out_specs=pl.BlockSpec(memory_space=pl.ANY),
        scratch_shapes=[
            vec(ncol * SROWS),
            vec(NWIN * WR), vec(NWIN * WR), vec(4 * WR), vec(4 * WR), vec(3 * WR), vec(3 * WR),
            pltpu.VMEM((2, NWIN, WR, WR), BF16), pltpu.VMEM((2, NWIN, WR, WR), BF16),
            sem((2, CHUNKS, reach)), sem((2, CHUNKS, reach)),
            sem((CHUNKS, nz)), sem((CHUNKS, nz)),
            sem((2, 2)), sem((2, 2)), sem((3,)),
        ],
        compiler_params=pltpu.CompilerParams(collective_id=0, has_side_effects=True),
        name="sweeps",
    )(offsets, refl.reshape(ROUNDS * 2 * NWIN, WR + NREF), evecs)
    start = WR - offsets[ROUNDS - 1, 1]
    return lax.dynamic_slice_in_dim(spread, start, NWIN * WR, 0)


def solution(mesh):
    placed = (P("row", "col"), P(), P(None, None, "row", "col", None))
    return jax.shard_map(
        shards, mesh=mesh, in_specs=placed, out_specs=P("row", "col"), check_vma=False
    )
```

time: 372 us -> 99.7 us (0.27)
  blocking collectives: 233 us -> 0 us
  Pallas kernels: 0 us -> 92.3 us
  waiting for transfers between devices: 49.2 us -> 0 us
  starting transfers between devices: 40 us -> 0 us
  between operations: 15.8 us -> 1.32 us
  matrix products: 14.2 us -> 0 us
  local copies, waits for them, and re-layouts: 12.2 us -> 4.92 us
  other arithmetic: 6.56 us -> 0.84 us
    all_gather x4 -> x0, blocking collectives: 233 us -> none  [shards(): blocks = lax.all_gather(refl[rnd], 'col', axis=2, tiled=True)]
    pallas_call x0 -> x1, Pallas kernels: none -> 92.3 us  [shards(): pl.pallas_call(functools.partial(kernel, nrow, nz), out_shape=jax.ShapeDt...]
    ppermute x16 -> x0, waiting for transfers between devices: 49.2 us -> none  [shifted(): return lax.ppermute(block, axis, route)]
    ppermute x16 -> x0, starting transfers between devices: 40 us -> none  [shifted(): return lax.ppermute(block, axis, route)]
    dot_general x24 -> x0, matrix products: 14.2 us -> none  [the longest x8 4.81 us: apply_blocks(): jnp.einsum('kjw,kjc->kwc', reflect, scaled, precision=lax.Precision.HIGHEST)]
    dynamic_update_slice x8 -> x0, local copies, waits for them, and re-layouts: 9.46 us -> none  [shards(): lax.dynamic_update_slice_in_dim(extended, updated.reshape(rows, cols), st...]
    and x8 -> x0, other arithmetic: 5.01 us -> none  [shards(): taking = (lines < start) & (place > 0)]
  transfers between devices with their start and end apart: 16 -> 0, of which waited for: 12 -> 0; matrix products, arithmetic and copies ran while one was open for 2% -> 0% of each run, Pallas kernels for 0% -> 0%
where the time goes in v1:
time: 99.7 us; the launch traced here: 99.4 us
  Pallas kernels  92.3 us (93%)
  local copies, waits for them, and re-layouts  4.92 us (5%)
  between operations  1.32 us (1%)
    pallas_call x1, Pallas kernels, shards(): pl.pallas_call(functools.partial(kernel, nrow, nz), out_shape=jax.ShapeDt...  92.3 us

profile of v1, /device:TPU:24, one launch (start us, length us, event | category | flops | bytes accessed | tf_op | source)
XLA Modules:
  0.0 99.4 jit_solution(13839240263344019702)
XLA Ops:
  0.0 1.3 %slice.3 = s32[1,1]{0,1:T(1,128)} slice(s32[4,2]{0,1:T(2,128)} %param.4), slice={[3:4], [1:2]} | slice | bytes 8 | tf_op jit(solution)/shard_map/slice | solution.py:331
  2.6 0.0 copy-start
  2.6 0.7 copy-done
  3.2 0.7 copy.4.off_ref
  3.9 0.8 reduce
  4.8 0.6 reshape.7.refl_ref
  5.4 92.3 %sweeps.1 = f32[640,128]{1,0:T(8,128)} custom-call(s32[4,2]{1,0:T(4,128)} %copy.4.off_ref, f32[32,192]{1,0:T(8,128)} %reshape.7.refl_ref, f32[512,128]{1,0:T(8,128)} %ev_ref.1), custom_call_target="tpu_custom_call" | custom-call | tf_op jit(solution)/shard_map/sweeps/pallas_call | solution.py:311
  97.7 1.7 %constant_dynamic-slice_fusion = f32[512,128]{1,0:T(8,128)} fusion(f32[640,128]{1,0:T(8,128)} %sweeps.1, s32[]{:T(128)S(6)} %select_n.3), kind=kLoop, calls=%fused_computation | loop fusion | bytes 524292 | tf_op jit(solution)/shard_map/dynamic_slice | solution.py:332
Async XLA Ops:
  2.6 0.7 copy-start

commit v2 on v1

--- a/solution.py
+++ b/solution.py
@@ -12,7 +12,7 @@
 ROUNDS = 4
 NWIN = 4
 NCOL = 128
-STRIDE = 2
+STRIDE = 4
 CHUNKS = 2
 CROWS = 24
 SROWS = CHUNKS * CROWS
@@ -35,9 +35,9 @@
 
 
 def kernel(
-    nrow, nz, off_ref, refl_ref, ev_ref, out_ref,
+    nrow, nz, off_hbm, refl_ref, ev_ref, out_ref,
     gath, own0, own1, lo0, lo1, hi0, hi1, hmat_hi, hmat_lo,
-    zsend, zrecv, psend, precv, xsend, xrecv, lsem,
+    zsend, zrecv, psend, precv, xsend, xrecv, lsem, off_ref,
 ):
     p = lax.axis_index("row")
     j = lax.axis_index("col")
@@ -65,17 +65,22 @@
         pltpu.make_async_copy(ev_ref, own0, lsem.at[0]),
         pltpu.make_async_copy(ev_ref.at[pl.ds(0, 2 * WR)], lo0.at[pl.ds(2 * WR, 2 * WR)], lsem.at[1]),
         pltpu.make_async_copy(ev_ref.at[pl.ds(2 * WR, 2 * WR)], hi0.at[pl.ds(0, 2 * WR)], lsem.at[2]),
+        pltpu.make_async_copy(off_hbm, off_ref, lsem.at[3]),
     ]
     for copy in local:
         copy.start()
 
+    def shard_rows(rnd, lanes):
+        return jnp.concatenate(
+            [refl_ref[rnd, sweep, w, :, lanes] for sweep in range(2) for w in range(NWIN)], 0
+        )
+
     def piece(rnd):
-        return refl_ref[pl.ds(8 * rnd, 8), :WR]
+        return shard_rows(rnd, slice(0, WR))
 
     def factors(rnd):
-        a = refl_ref[pl.ds(8 * rnd, 8), WR:]
-        b = refl_ref[pl.ds(8 * rnd + 8, 8), WR:]
-        return jnp.concatenate([a, b], 1)
+        lanes = slice(WR, WR + NREF)
+        return jnp.concatenate([shard_rows(rnd, lanes), shard_rows(rnd + 1, lanes)], 1)
 
     base = pl.multiple_of(j * SROWS, 8)
     for tile, value in enumerate((piece(0), factors(0), piece(1), piece(2), factors(2), piece(3))):
@@ -155,48 +160,47 @@
     def far(way, q):
         return nz // 2 if way == q else nz // 2 - 1
 
-    def reaches(d, way, q, last):
-        order = [STRIDE] + list(range(1, STRIDE))
-        return [r for r in order if not last or d + r <= far(way, q)]
-
-    def relay(d, last):
-        for q in range(CHUNKS):
-            for way in range(2):
-                if not isinstance(d, int) or d > 0:
+    def relay(d, q):
+        for way in range(2):
+            if d:
+                arrival(way, d, q).wait_recv()
+            for r in [STRIDE] + list(range(1, STRIDE)):
+                if d + r <= far(way, q):
+                    hop(way, d, q, r).start()
+        for way in range(2 if d else 1):
+            across(chip((2 * way - 1) * d), q).start()
+
+    def settle(first, q):
+        for way in range(2):
+            for d in range(first, first + STRIDE):
+                if d % STRIDE and d <= far(way, q) or d == nz // 2 == far(way, q):
                     arrival(way, d, q).wait_recv()
-                for r in reaches(d, way, q, last):
-                    hop(way, d, q, r).start()
-            if isinstance(d, int) and d == 0:
-                across(z, q).start()
-            else:
-                for way in range(2):
                     across(chip((2 * way - 1) * d), q).start()
 
-    def settle_step(d):
-        for q in range(CHUNKS):
-            for way in range(2):
-                for r in range(1, STRIDE):
-                    arrival(way, d + r, q).wait_recv()
-                    across(chip((2 * way - 1) * (d + r)), q).start()
-
-    half = nz // 2
-    last_relay = half - STRIDE
-    relay(0, last_relay == 0)
-
-    def step(m, carry):
-        relay(m * STRIDE, False)
-        settle_step((m - 1) * STRIDE)
-        return carry
-
-    lax.fori_loop(1, last_relay // STRIDE, step, 0)
-    relay(last_relay, True)
-    if last_relay:
-        settle_step(last_relay - STRIDE)
-    for q in range(CHUNKS):
-        for way in range(2):
-            for d in range(last_relay + 1, far(way, q) + 1):
-                arrival(way, d, q).wait_recv()
-                across(chip((2 * way - 1) * d), q).start()
+    relays = range(0, nz // 2, STRIDE)
+
+    def steps_of(q):
+        steps = []
+        for d in relays:
+            steps.append([functools.partial(relay, d, q)])
+            if d:
+                steps[-1].append(functools.partial(settle, d - STRIDE + 1, q))
+        steps.append([functools.partial(settle, relays[-1] + 1, q)])
+        return steps
+
+    early, late = steps_of(0), steps_of(1)
+
+    def run(step):
+        for part in step:
+            part()
+
+    behind = len(early) - 3
+    for i, step in enumerate(early):
+        step[0]()
+        if 0 <= i - behind and i < len(early) - 1:
+            late.pop(0)[0]() if i == behind else run(late.pop(0))
+        for part in step[1:]:
+            part()
 
     def partner_done(q):
         def body(i, carry):
@@ -230,7 +234,7 @@
         return dot3((hmat_hi[t % 2, w], hmat_lo[t % 2, w]), e, ((1,), (0,)))
 
     def offset(t):
-        return off_ref[(t - 1) // 2, (t - 1) % 2] if t else 0
+        return off_ref[(t - 1) % 2, (t - 1) // 2] if t else 0
 
     lines = lax.broadcasted_iota(jnp.int32, (WR, NCOL), 0)
     partner_done(0)
@@ -245,6 +249,8 @@
                 lo[new][pl.ds(3 * WR, WR), :] = got
             else:
                 hi[new][pl.ds(0, WR), :] = got
+        if late:
+            run(late.pop(0))
         if t == ROUNDS:
             partner_done(1)
         if t < 2 * ROUNDS:
@@ -276,10 +282,15 @@
 
     final = 2 * ROUNDS
     par = final % 2
-    tail = pltpu.make_async_copy(own[par], out_ref.at[pl.ds(WR, NWIN * WR)], lsem.at[0])
+    result = own[1 - par]
+    result[pl.ds(WR, 3 * WR), :] = own[par][pl.ds(WR - offset(final), 3 * WR), :]
+    tail = pltpu.make_async_copy(
+        result.at[pl.ds(WR, 3 * WR)], out_ref.at[pl.ds(WR, 3 * WR)], lsem.at[0]
+    )
     tail.start()
     if_below(lambda: up(final).wait_recv())
-    head = pltpu.make_async_copy(lo[par].at[pl.ds(WR, WR)], out_ref.at[pl.ds(0, WR)], lsem.at[1])
+    result[pl.ds(0, WR), :] = lo[par][pl.ds(2 * WR - offset(final), WR), :]
+    head = pltpu.make_async_copy(result.at[pl.ds(0, WR)], out_ref.at[pl.ds(0, WR)], lsem.at[1])
     head.start()
 
     if_below(lambda: down(final - 1).wait_send())
@@ -308,11 +319,11 @@
     vec = lambda rows: pltpu.VMEM((rows, NCOL), F32)
     sem = pltpu.SemaphoreType.DMA
     reach = nz // 2 + 1
-    spread = pl.pallas_call(
+    return pl.pallas_call(
         functools.partial(kernel, nrow, nz),
-        out_shape=jax.ShapeDtypeStruct(((NWIN + 1) * WR, NCOL), F32),
+        out_shape=jax.ShapeDtypeStruct((NWIN * WR, NCOL), F32),
         in_specs=[
-            pl.BlockSpec(memory_space=pltpu.SMEM),
+            pl.BlockSpec(memory_space=pl.ANY),
             pl.BlockSpec(memory_space=pltpu.VMEM),
             pl.BlockSpec(memory_space=pl.ANY),
         ],
@@ -323,13 +334,12 @@
             pltpu.VMEM((2, NWIN, WR, WR), BF16), pltpu.VMEM((2, NWIN, WR, WR), BF16),
             sem((2, CHUNKS, reach)), sem((2, CHUNKS, reach)),
             sem((CHUNKS, nz)), sem((CHUNKS, nz)),
-            sem((2, 2)), sem((2, 2)), sem((3,)),
+            sem((2, 2)), sem((2, 2)), sem((4,)),
+            pltpu.SMEM((2, ROUNDS), jnp.int32),
         ],
         compiler_params=pltpu.CompilerParams(collective_id=0, has_side_effects=True),
         name="sweeps",
-    )(offsets, refl.reshape(ROUNDS * 2 * NWIN, WR + NREF), evecs)
-    start = WR - offsets[ROUNDS - 1, 1]
-    return lax.dynamic_slice_in_dim(spread, start, NWIN * WR, 0)
+    )(offsets.T, refl, evecs)
 
 
 def solution(mesh):

time: 99.7 us -> 88.7 us (0.89)
  Pallas kernels: 92.3 us -> 86.8 us
  local copies, waits for them, and re-layouts: 4.92 us -> 1.67 us
  between operations: 1.32 us -> 0.01 us
    pallas_call x1, Pallas kernels: 92.3 us -> 86.8 us  [shards(): pl.pallas_call(functools.partial(kernel, nrow, nz), out_shape=jax.ShapeDt...]
    dynamic_slice x1 -> x0, local copies, waits for them, and re-layouts: 1.69 us -> none  [shards(): return lax.dynamic_slice_in_dim(spread, start, NWIN * WR, 0)]
    slice x1 -> x0, local copies, waits for them, and re-layouts: 1.26 us -> none  [shards(): start = WR - offsets[ROUNDS - 1, 1]]
where the time goes in v2:
time: 88.7 us; the launch traced here: 88.5 us
  Pallas kernels  86.8 us (98%)
  local copies, waits for them, and re-layouts  1.67 us (2%)
    pallas_call x1, Pallas kernels, shards(): pl.pallas_call(functools.partial(kernel, nrow, nz), out_shape=jax.ShapeDt...  86.8 us

profile of v2, /device:TPU:24, one launch (start us, length us, event | category | flops | bytes accessed | tf_op | source)
XLA Modules:
  0.0 88.5 jit_solution(6433089418113711997)
XLA Ops:
  0.0 86.8 %sweeps.1 = f32[512,128]{1,0:T(8,128)} custom-call(s32[2,4]{1,0:T(2,128)} %bitcast.1, f32[4,2,4,1,192]{4,3,2,1,0:T(1,128)} %refl_ref.1, f32[512,128]{1,0:T(8,128)} %ev_ref.1), custom_call_target="tpu_custom_call" | custom-call | tf_op jit(solution)/shard_map/sweeps/pallas_call | solution.py:322
  86.8 1.7 %copy.5 = f32[512,128]{1,0:T(8,128)} copy(f32[512,128]{1,0:T(8,128)} %sweeps.1) | data formatting | bytes 524288

commit v3 on v2

--- a/solution.py
+++ b/solution.py
@@ -12,6 +12,8 @@
 ROUNDS = 4
 NWIN = 4
 NCOL = 128
+OWN = NWIN * WR
+BELOW = 3 * WR
 STRIDE = 4
 CHUNKS = 2
 CROWS = 24
@@ -36,14 +38,14 @@
 
 def kernel(
     nrow, nz, off_hbm, refl_ref, ev_ref, out_ref,
-    gath, own0, own1, lo0, lo1, hi0, hi1, hmat_hi, hmat_lo,
-    zsend, zrecv, psend, precv, xsend, xrecv, lsem, off_ref,
+    gath, state0, state1, mid, last, sent, got, first_hi, first_lo, second_hi, second_lo,
+    zsend, zrecv, psend, precv, xsend, xrecv, hsend, hrecv, lsem, off_ref,
 ):
     p = lax.axis_index("row")
     j = lax.axis_index("col")
     z, c = j // 2, j % 2
     partner = z * 2 + (1 - c)
-    own, lo, hi = (own0, own1), (lo0, lo1), (hi0, hi1)
+    state = (state0, state1)
 
     def chip(d):
         return lax.rem(z + d + 2 * nz, nz)
@@ -62,10 +64,8 @@
         pl.semaphore_signal(barrier, inc=1, device_id={"row": p + 1}, device_id_type=MESH)
 
     local = [
-        pltpu.make_async_copy(ev_ref, own0, lsem.at[0]),
-        pltpu.make_async_copy(ev_ref.at[pl.ds(0, 2 * WR)], lo0.at[pl.ds(2 * WR, 2 * WR)], lsem.at[1]),
-        pltpu.make_async_copy(ev_ref.at[pl.ds(2 * WR, 2 * WR)], hi0.at[pl.ds(0, 2 * WR)], lsem.at[2]),
-        pltpu.make_async_copy(off_hbm, off_ref, lsem.at[3]),
+        pltpu.make_async_copy(ev_ref, state0.at[pl.ds(BELOW, OWN)], lsem.at[0]),
+        pltpu.make_async_copy(off_hbm, off_ref, lsem.at[1]),
     ]
     for copy in local:
         copy.start()
@@ -85,34 +85,51 @@
     base = pl.multiple_of(j * SROWS, 8)
     for tile, value in enumerate((piece(0), factors(0), piece(1), piece(2), factors(2), piece(3))):
         gath[pl.ds(base + 8 * tile, 8), :value.shape[1]] = value
+    eye = (
+        lax.broadcasted_iota(jnp.int32, (WR, WR), 0) == lax.broadcasted_iota(jnp.int32, (WR, WR), 1)
+    ).astype(F32)
+
     for par in range(2):
-        lo[par][pl.ds(0, WR), :] = jnp.zeros((WR, NCOL), F32)
+        state[par][pl.ds(0, WR), :] = jnp.zeros((WR, NCOL), F32)
 
     @pl.when(p == 0)
     def _():
         for par in range(2):
-            lo[par][pl.ds(WR, WR), :] = jnp.zeros((WR, NCOL), F32)
+            state[par][pl.ds(WR, 2 * WR), :] = jnp.zeros((2 * WR, NCOL), F32)
+        for rnd in range(ROUNDS):
+            got[rnd, 0] = eye
 
     @pl.when(p == nrow - 1)
     def _():
         for par in range(2):
-            hi[par][pl.ds(2 * WR, WR), :] = jnp.zeros((WR, NCOL), F32)
+            state[par][pl.ds(BELOW + OWN, 2 * WR), :] = jnp.zeros((2 * WR, NCOL), F32)
+        for rnd in range(ROUNDS):
+            got[rnd, 1] = eye
 
     pl.semaphore_wait(barrier, 2 * STRIDE + 1 + (p > 0).astype(jnp.int32) + (p < nrow - 1).astype(jnp.int32))
 
-    def down(t):
-        par = t % 2
-        src = ev_ref.at[pl.ds(0, WR)] if t == 0 else lo[par].at[pl.ds(2 * WR, WR)]
-        return pltpu.make_async_remote_copy(
-            src, hi[par].at[pl.ds(2 * WR, WR)], xsend.at[0, par], xrecv.at[0, par],
+    def down(r):
+        par = r % 2
+        src = ev_ref.at[pl.ds(0, 2 * WR)] if r == 0 else state[par].at[pl.ds(BELOW, 2 * WR)]
+        return pltpu.make_async_remote_copy(
+            src, state[par].at[pl.ds(BELOW + OWN, 2 * WR)], xsend.at[0, par], xrecv.at[0, par],
             device_id={"row": p - 1}, device_id_type=MESH,
         )
 
-    def up(t):
-        par = t % 2
-        return pltpu.make_async_remote_copy(
-            hi[par].at[pl.ds(WR, WR)], lo[par].at[pl.ds(WR, WR)], xsend.at[1, par], xrecv.at[1, par],
+    def up(r):
+        par = r % 2
+        size = WR if r == ROUNDS else 2 * WR
+        at = BELOW + OWN - size
+        src = ev_ref.at[pl.ds(OWN - size, size)] if r == 0 else state[par].at[pl.ds(at, size)]
+        return pltpu.make_async_remote_copy(
+            src, state[par].at[pl.ds(BELOW - size, size)], xsend.at[1, par], xrecv.at[1, par],
             device_id={"row": p + 1}, device_id_type=MESH,
+        )
+
+    def share(rnd, side):
+        return pltpu.make_async_remote_copy(
+            sent.at[rnd, side], got.at[rnd, side], hsend.at[rnd, side], hrecv.at[rnd, side],
+            device_id={"row": p - 1 if side else p + 1}, device_id_type=MESH,
         )
 
     def if_below(f):
@@ -122,6 +139,7 @@
         pl.when(p < nrow - 1)(f)
 
     if_below(lambda: down(0).start())
+    if_above(lambda: up(0).start())
 
     def rows_of(chip_index, core, q):
         at = (chip_index * 2 + core) * SROWS + q * CROWS
@@ -211,91 +229,116 @@
     for copy in local:
         copy.wait()
 
-    eye = (
-        lax.broadcasted_iota(jnp.int32, (WR, WR), 0) == lax.broadcasted_iota(jnp.int32, (WR, WR), 1)
-    ).astype(F32)
-
-    def build(t):
-        rnd, sweep = t // 2, t % 2
+    def window(rnd, sweep, w):
         vtile = (0, 2, 3, 5)[rnd]
         ttile = (1, 1, 4, 4)[rnd]
+        row = sweep * NWIN + w
+        vt = split(gath[pl.ds(8 * vtile + row, NREF, stride=SROWS), :])
+        packed = gath[pl.ds(8 * ttile + row, NREF, stride=SROWS), :]
+        tf = split(packed[:, NREF * (rnd % 2):NREF * (rnd % 2) + NREF])
+        tv = split(dot3(tf, vt, ((1,), (0,))))
+        return eye - dot3(vt, tv, ((0,), (0,)))
+
+    def keep(his, los, at, value):
+        his[at], los[at] = split(value)
+
+    def build_outer(rnd):
+        sent[rnd, 0] = window(rnd, 0, NWIN - 1)
+        if_above(lambda: share(rnd, 0).start())
+        sent[rnd, 1] = window(rnd, 0, 0)
+        if_below(lambda: share(rnd, 1).start())
+
+    def build(rnd):
+        keep(first_hi, first_lo, NWIN, sent[rnd, 0])
+        keep(first_hi, first_lo, 1, sent[rnd, 1])
+        for w in range(1, NWIN - 1):
+            keep(first_hi, first_lo, w + 1, window(rnd, 0, w))
         for w in range(NWIN):
-            row = sweep * NWIN + w
-            vt = split(gath[pl.ds(8 * vtile + row, NREF, stride=SROWS), :])
-            packed = gath[pl.ds(8 * ttile + row, NREF, stride=SROWS), :]
-            tf = split(packed[:, NREF * (rnd % 2):NREF * (rnd % 2) + NREF])
-            tv = split(dot3(tf, vt, ((1,), (0,))))
-            h, l = split(eye - dot3(vt, tv, ((0,), (0,))))
-            hmat_hi[t % 2, w] = h
-            hmat_lo[t % 2, w] = l
-
-    def apply(t, w, rows):
-        e = split(rows)
-        return dot3((hmat_hi[t % 2, w], hmat_lo[t % 2, w]), e, ((1,), (0,)))
+            keep(second_hi, second_lo, w, window(rnd, 1, w))
 
     def offset(t):
         return off_ref[(t - 1) % 2, (t - 1) // 2] if t else 0
 
     lines = lax.broadcasted_iota(jnp.int32, (WR, NCOL), 0)
+    end = jnp.where(p == nrow - 1, OWN, 2 * OWN)
+
     partner_done(0)
+    build_outer(0)
     build(0)
-    for t in range(1, 2 * ROUNDS + 1):
-        old, new = (t - 1) % 2, t % 2
-        shift = offset(t) - offset(t - 1)
-        for w in (1, 2):
-            got = apply(t - 1, w, own[old][pl.ds(shift + WR * w, WR), :])
-            own[new][pl.ds(WR * w, WR), :] = got
-            if w == 1:
-                lo[new][pl.ds(3 * WR, WR), :] = got
-            else:
-                hi[new][pl.ds(0, WR), :] = got
-        if late:
-            run(late.pop(0))
-        if t == ROUNDS:
-            partner_done(1)
-        if t < 2 * ROUNDS:
-            build(t)
-        if_above(lambda: down(t - 1).wait_recv())
-        if t > 1:
-            if_below(lambda: up(t - 1).wait_recv())
-        if t > 2:
-            if_below(lambda: down(t - 2).wait_send())
-            if_above(lambda: up(t - 2).wait_send())
-        elif t == 2:
-            if_below(lambda: down(0).wait_send())
+    build_outer(1)
+    for rnd in range(ROUNDS):
+        old, new = rnd % 2, (rnd + 1) % 2
+        before, a, b = offset(2 * rnd), offset(2 * rnd + 1), offset(2 * rnd + 2)
+        extra = (b < a).astype(jnp.int32)
+        low = a - WR * extra
+        if rnd:
+            build(rnd)
+            if rnd == 2:
+                build_outer(3)
+        if_below(lambda: up(rnd).wait_recv())
+        if_above(lambda: down(rnd).wait_recv())
+        if_below(lambda: share(rnd, 0).wait_recv())
+        if_above(lambda: share(rnd, 1).wait_recv())
+        keep(first_hi, first_lo, 0, got[rnd, 0])
+        keep(first_hi, first_lo, NWIN + 1, got[rnd, 1])
 
         @pl.when(p == 0)
         def _():
-            lo[new][pl.ds(WR, WR), :] = lo[old][pl.ds(shift + WR, WR), :]
-
-        got = apply(t - 1, 0, lo[old][pl.ds(shift + 2 * WR, WR), :])
-        lo[new][pl.ds(2 * WR, WR), :] = got
-        if t < 2 * ROUNDS:
-            if_below(lambda: down(t).start())
-        own[new][pl.ds(0, WR), :] = got
-        got = apply(t - 1, 3, hi[old][pl.ds(shift + WR, WR), :])
-        limit = jnp.where(p == nrow - 1, WR - offset(t), WR)
-        got = jnp.where(lines < limit, got, 0.0)
-        hi[new][pl.ds(WR, WR), :] = got
-        if_above(lambda: up(t).start())
-        own[new][pl.ds(3 * WR, WR), :] = got
-
-    final = 2 * ROUNDS
-    par = final % 2
-    result = own[1 - par]
-    result[pl.ds(WR, 3 * WR), :] = own[par][pl.ds(WR - offset(final), 3 * WR), :]
+            mid[pl.ds(0, WR), :] = state[old][pl.ds(BELOW - WR + low - before, WR), :]
+
+        for i in range(NWIN + 1):
+            e = split(state[old][pl.ds(BELOW + WR * i + low - before, WR), :])
+            k = i + 1 - extra
+            value = dot3((first_hi[k], first_lo[k]), e, ((1,), (0,)))
+            if i >= NWIN - 1:
+                value = jnp.where(lines < end - low - WR * i, value, 0.0)
+            mid[pl.ds(WR * (i + 1), WR), :] = value
+        if rnd:
+            if_below(lambda: down(rnd - 1).wait_send())
+            if_above(lambda: up(rnd - 1).wait_send())
+        for w in (3, 2, 0, 1):
+            e = split(mid[pl.ds(WR * (w + 1) + b - low, WR), :])
+            value = dot3((second_hi[w], second_lo[w]), e, ((1,), (0,)))
+            if w == NWIN - 1:
+                value = jnp.where(lines < end - b - WR * w, value, 0.0)
+            state[new][pl.ds(BELOW + WR * w, WR), :] = value
+            if rnd == ROUNDS - 1:
+                last[pl.ds(WR * w, WR), :] = value
+            if w == (3 if rnd == ROUNDS - 1 else 2):
+                if_above(lambda: up(rnd + 1).start())
+        if rnd < ROUNDS - 1:
+            if_below(lambda: down(rnd + 1).start())
+
+        @pl.when(p == 0)
+        def _():
+            state[new][pl.ds(BELOW - WR, WR), :] = mid[pl.ds(b - low, WR), :]
+
+        if rnd == 0:
+            while late:
+                run(late.pop(0))
+        if rnd == 1:
+            partner_done(1)
+            build_outer(2)
+
+    par = ROUNDS % 2
+    result = mid
+    shift = BELOW - offset(2 * ROUNDS)
+    result[pl.ds(WR, 3 * WR), :] = last[pl.ds(WR - offset(2 * ROUNDS), 3 * WR), :]
     tail = pltpu.make_async_copy(
         result.at[pl.ds(WR, 3 * WR)], out_ref.at[pl.ds(WR, 3 * WR)], lsem.at[0]
     )
     tail.start()
-    if_below(lambda: up(final).wait_recv())
-    result[pl.ds(0, WR), :] = lo[par][pl.ds(2 * WR - offset(final), WR), :]
+    if_below(lambda: up(ROUNDS).wait_recv())
+    result[pl.ds(0, WR), :] = state[par][pl.ds(shift, WR), :]
     head = pltpu.make_async_copy(result.at[pl.ds(0, WR)], out_ref.at[pl.ds(0, WR)], lsem.at[1])
     head.start()
 
-    if_below(lambda: down(final - 1).wait_send())
-    if_above(lambda: up(final - 1).wait_send())
-    if_above(lambda: up(final).wait_send())
+    if_below(lambda: down(ROUNDS - 1).wait_send())
+    if_above(lambda: up(ROUNDS - 1).wait_send())
+    if_above(lambda: up(ROUNDS).wait_send())
+    for rnd in range(ROUNDS):
+        if_above(lambda: share(rnd, 0).wait_send())
+        if_below(lambda: share(rnd, 1).wait_send())
 
     def drain(i, carry):
         for q in range(CHUNKS):
@@ -330,11 +373,13 @@
         out_specs=pl.BlockSpec(memory_space=pl.ANY),
         scratch_shapes=[
             vec(ncol * SROWS),
-            vec(NWIN * WR), vec(NWIN * WR), vec(4 * WR), vec(4 * WR), vec(3 * WR), vec(3 * WR),
-            pltpu.VMEM((2, NWIN, WR, WR), BF16), pltpu.VMEM((2, NWIN, WR, WR), BF16),
+            vec(BELOW + OWN + 2 * WR), vec(BELOW + OWN + 2 * WR), vec((NWIN + 2) * WR), vec(OWN),
+            pltpu.VMEM((ROUNDS, 2, WR, WR), F32), pltpu.VMEM((ROUNDS, 2, WR, WR), F32),
+            pltpu.VMEM((NWIN + 2, WR, WR), BF16), pltpu.VMEM((NWIN + 2, WR, WR), BF16),
+            pltpu.VMEM((NWIN, WR, WR), BF16), pltpu.VMEM((NWIN, WR, WR), BF16),
             sem((2, CHUNKS, reach)), sem((2, CHUNKS, reach)),
             sem((CHUNKS, nz)), sem((CHUNKS, nz)),
-            sem((2, 2)), sem((2, 2)), sem((4,)),
+            sem((2, 2)), sem((2, 2)), sem((ROUNDS, 2)), sem((ROUNDS, 2)), sem((2,)),
             pltpu.SMEM((2, ROUNDS), jnp.int32),
         ],
         compiler_params=pltpu.CompilerParams(collective_id=0, has_side_effects=True),

time: 88.7 us -> 82.3 us (0.928)
  Pallas kernels: 86.8 us -> 79.5 us
    pallas_call x1, Pallas kernels: 86.8 us -> 79.5 us  [shards(): pl.pallas_call(functools.partial(kernel, nrow, nz), out_shape=jax.ShapeDt...]
where the time goes in v3:
time: 82.3 us; the launch traced here: 81.2 us
  Pallas kernels  79.5 us (97%)
  local copies, waits for them, and re-layouts  1.67 us (2%)
    pallas_call x1, Pallas kernels, shards(): pl.pallas_call(functools.partial(kernel, nrow, nz), out_shape=jax.ShapeDt...  79.5 us
    unnamed x1, local copies, waits for them, and re-layouts  1.67 us

profile of v3, /device:TPU:24, one launch (start us, length us, event | category | flops | bytes accessed | tf_op | source)
XLA Modules:
  0.0 81.2 jit_solution(4352729395799981273)
XLA Ops:
  0.0 79.5 %sweeps.1 = f32[512,128]{1,0:T(8,128)} custom-call(s32[2,4]{1,0:T(2,128)} %bitcast.1, f32[4,2,4,1,192]{4,3,2,1,0:T(1,128)} %refl_ref.1, f32[512,128]{1,0:T(8,128)} %ev_ref.1), custom_call_target="tpu_custom_call" | custom-call | tf_op jit(solution)/shard_map/sweeps/pallas_call | solution.py:365
  79.5 1.7 %copy.5 = f32[512,128]{1,0:T(8,128)} copy(f32[512,128]{1,0:T(8,128)} %sweeps.1) | data formatting | bytes 524288

commit v4 on v3

--- a/solution.py
+++ b/solution.py
@@ -14,8 +14,9 @@
 NCOL = 128
 OWN = NWIN * WR
 BELOW = 3 * WR
-STRIDE = 4
 CHUNKS = 2
+STRIDES = (4, 4)
+PLAN = (0, 1, 1, 1, 1, 1, 0)
 CROWS = 24
 SROWS = CHUNKS * CROWS
 MESH = pl.DeviceIdType.MESH
@@ -51,7 +52,7 @@
         return lax.rem(z + d + 2 * nz, nz)
 
     barrier = pltpu.get_barrier_semaphore()
-    for d in [x for x in range(-STRIDE, STRIDE + 1) if x]:
+    for d in [x for x in range(-max(STRIDES), max(STRIDES) + 1) if x]:
         pl.semaphore_signal(barrier, inc=1, device_id={"col": chip(d) * 2 + c}, device_id_type=MESH)
     pl.semaphore_signal(barrier, inc=1, device_id={"col": partner}, device_id_type=MESH)
 
@@ -106,7 +107,7 @@
         for rnd in range(ROUNDS):
             got[rnd, 1] = eye
 
-    pl.semaphore_wait(barrier, 2 * STRIDE + 1 + (p > 0).astype(jnp.int32) + (p < nrow - 1).astype(jnp.int32))
+    pl.semaphore_wait(barrier, 2 * max(STRIDES) + 1 + (p > 0).astype(jnp.int32) + (p < nrow - 1).astype(jnp.int32))
 
     def down(r):
         par = r % 2
@@ -182,7 +183,7 @@
         for way in range(2):
             if d:
                 arrival(way, d, q).wait_recv()
-            for r in [STRIDE] + list(range(1, STRIDE)):
+            for r in [STRIDES[q]] + list(range(1, STRIDES[q])):
                 if d + r <= far(way, q):
                     hop(way, d, q, r).start()
         for way in range(2 if d else 1):
@@ -190,19 +191,17 @@
 
     def settle(first, q):
         for way in range(2):
-            for d in range(first, first + STRIDE):
-                if d % STRIDE and d <= far(way, q) or d == nz // 2 == far(way, q):
+            for d in range(first, first + STRIDES[q]):
+                if d % STRIDES[q] and d <= far(way, q) or d == nz // 2 == far(way, q):
                     arrival(way, d, q).wait_recv()
                     across(chip((2 * way - 1) * d), q).start()
 
-    relays = range(0, nz // 2, STRIDE)
-
     def steps_of(q):
-        steps = []
+        steps, relays = [], range(0, nz // 2, STRIDES[q])
         for d in relays:
             steps.append([functools.partial(relay, d, q)])
             if d:
-                steps[-1].append(functools.partial(settle, d - STRIDE + 1, q))
+                steps[-1].append(functools.partial(settle, d - STRIDES[q] + 1, q))
         steps.append([functools.partial(settle, relays[-1] + 1, q)])
         return steps
 
@@ -212,13 +211,15 @@
         for part in step:
             part()
 
-    behind = len(early) - 3
+    def run_late(point):
+        for _ in range(PLAN[point]):
+            if late:
+                run(late.pop(0))
+
     for i, step in enumerate(early):
-        step[0]()
-        if 0 <= i - behind and i < len(early) - 1:
-            late.pop(0)[0]() if i == behind else run(late.pop(0))
-        for part in step[1:]:
-            part()
+        run(step)
+        if i < len(early) - 1:
+            run_late(i)
 
     def partner_done(q):
         def body(i, carry):
@@ -264,6 +265,7 @@
 
     partner_done(0)
     build_outer(0)
+    run_late(4)
     build(0)
     build_outer(1)
     for rnd in range(ROUNDS):
@@ -313,10 +315,11 @@
         def _():
             state[new][pl.ds(BELOW - WR, WR), :] = mid[pl.ds(b - low, WR), :]
 
-        if rnd == 0:
+        if rnd < 2:
+            run_late(5 + rnd)
+        if rnd == 1:
             while late:
                 run(late.pop(0))
-        if rnd == 1:
             partner_done(1)
             build_outer(2)
 

time: 82.3 us -> 78.6 us (0.955); the launches traced: 81.2 us -> 78.3 us
  Pallas kernels: 79.5 us -> 76.6 us
    pallas_call x1, Pallas kernels: 79.5 us -> 76.6 us  [shards(): pl.pallas_call(functools.partial(kernel, nrow, nz), out_shape=jax.ShapeDt...]
where the time goes in v4:
time: 78.6 us; the launch traced here: 78.3 us
  Pallas kernels  76.6 us (97%)
  local copies, waits for them, and re-layouts  1.67 us (2%)
    pallas_call x1, Pallas kernels, shards(): pl.pallas_call(functools.partial(kernel, nrow, nz), out_shape=jax.ShapeDt...  76.6 us
    unnamed x1, local copies, waits for them, and re-layouts  1.67 us

profile of v4, /device:TPU:24, one launch (start us, length us, event | category | flops | bytes accessed | tf_op | source)
XLA Modules:
  0.0 78.3 jit_solution(1862733876291248705)
XLA Ops:
  0.0 76.6 %sweeps.1 = f32[512,128]{1,0:T(8,128)} custom-call(s32[2,4]{1,0:T(2,128)} %bitcast.1, f32[4,2,4,1,192]{4,3,2,1,0:T(1,128)} %refl_ref.1, f32[512,128]{1,0:T(8,128)} %ev_ref.1), custom_call_target="tpu_custom_call" | custom-call | tf_op jit(solution)/shard_map/sweeps/pallas_call | solution.py:368
  76.7 1.7 %copy.5 = f32[512,128]{1,0:T(8,128)} copy(f32[512,128]{1,0:T(8,128)} %sweeps.1) | data formatting | bytes 524288
